TPU v7x, 256 devices: a whole 4x4x8 slice. The times are simulated.
256 devices in a mesh: slab: 4 (over x), row: 64 (over y, z, core).
Axes of the slice: x: 4, y: 4, z: 8, core: 2. Of those that a mesh axis runs over, the one named last changes fastest.
Arguments:
- forcing: bfloat16 [4, 32768, 64], P('slab', 'row'), may hold values from -6 to 6
- inflow: bfloat16 [32768, 64], P('row'), may hold values from -6 to 6
- self_solve: bfloat16 [4, 64, 512, 512], P('slab', 'row'), may hold values from -0.25 to 0.25
- greens: bfloat16 [4, 64, 20, 512, 512], P('slab', 'row'), may hold values from -0.078125 to 0.078125
- kept_cols: int32 [4, 64, 20], P('slab', 'row'), may hold values from 0 to 63, as said below
- counts: int32 [4, 64], P('slab', 'row'), may hold values from 6 to 20, as said below
Outputs:
- traces: bfloat16 [4, 32768, 64], P('slab', 'row')
Inputs may be any that keep to these rules, and one draw needn't show every extreme that they name: `kept_cols`: for each slab and tile row the 20 entries name distinct column tiles. `counts`: in every slab some tile row uses all 20 slots.
All inputs are finite; a program needn't handle non-finite values.
Results may differ from a plain program's by a relative error of at most 0.012.
Values may be sent and summed in bfloat16 or wider, within the bound.
A program may use at most 64 MiB of HBM per device.

v0:
```python
import jax
import jax.numpy as jnp
from jax import lax
from jax.sharding import PartitionSpec as P

TILE = 512


def shifted(array, axis, by):
    size = lax.axis_size(axis)
    pairs = [(i, i + by) for i in range(size) if 0 <= i + by < size]
    return lax.ppermute(array, axis, pairs)


def advance(previous, inflow_cols, forcing_cols, green_row, cols_row, count_row, solve_row):
    arrived = shifted(previous, "slab", 1)
    first_slab = lax.axis_index("slab") == 0
    incoming = jnp.where(first_slab, inflow_cols, arrived)
    gathered = lax.all_gather(incoming, "row", axis=0, tiled=True)
    width = incoming.shape[1]
    tiles = gathered.reshape(-1, TILE, width)
    chosen = tiles[cols_row]
    slot_ids = jnp.arange(green_row.shape[0], dtype=jnp.int32)
    valid = slot_ids < count_row
    chosen = jnp.where(valid[:, None, None], chosen, jnp.zeros((), chosen.dtype))
    total = jnp.einsum("kij,kjw->iw", green_row, chosen, preferred_element_type=jnp.float32)
    coupled = (total + forcing_cols.astype(jnp.float32)).astype(jnp.bfloat16)
    return jnp.dot(solve_row, coupled, preferred_element_type=jnp.float32).astype(jnp.bfloat16)


def shards(forcing, inflow, self_solve, greens, kept_cols, counts):
    slab_count = lax.axis_size("slab")
    green_row = greens[0, 0]
    cols_row = kept_cols[0, 0]
    count_row = counts[0, 0]
    solve_row = self_solve[0, 0]
    source = forcing[0]
    columns = source.shape[1]
    previous = jnp.zeros((TILE, columns), jnp.bfloat16)
    for section in range(slab_count):
        previous = advance(previous, inflow, source, green_row, cols_row, count_row, solve_row)
    return previous[None]


def solution(mesh):
    placed = (
        P("slab", "row", None),
        P("row", None),
        P("slab", "row", None, None),
        P("slab", "row", None, None, None),
        P("slab", "row", None),
        P("slab", "row"),
    )
    return jax.shard_map(
        shards, mesh=mesh, in_specs=placed, out_specs=P("slab", "row", None), check_vma=False
    )
```

profile of v0, /device:TPU:7, one launch (start us, length us, event | category | flops | bytes accessed | tf_op | source)
XLA Modules:
  0.0 407.8 jit_solution(2446877907097513772)
XLA Ops:
  6.5 0.0 copy-start
  6.5 0.0 all-gather.5.cloned.1.call-start
  6.5 1.4 collective-permute-start
  8.0 3.7 collective-permute-done
  11.7 0.6 broadcast_select_fusion.3
  12.3 0.0 all-gather.5.cloned.1.call-update
  12.4 0.0 all-gather.7.cloned.1.call-start
  13.1 0.7 fusion.156
  13.7 79.2 %all-gather.5.cloned.1.call-done = bf16[32768,64]{0,1:T(8,128)(2,1)} async-done(((bf16[512,64]{0,1:T(8,128)(2,1)}), bf16[32768,64]{0,1:T(8,128)(2,1)}) %all-gather.5.cloned.1.call-update) | async-done | bytes 4194320 | tf_op jit(solution)/shard_map/all_gather | solution.py:19
  93.0 4.8 %copy.22 = bf16[8,64,8,512]{3,2,0,1:T(8,128)(2,1)} copy(bf16[8,64,8,512]{3,2,1,0:T(8,128)(2,1)} %bitcast.176) | data formatting | bytes 8388608 | tf_op jit(solution)/shard_map/reshape | solution.py:21
  97.8 0.0 copy-start.1
  97.8 2.8 gather_fusion
  100.6 0.0 copy-done
  100.6 0.0 copy-done.1
  100.6 0.0 copy-start.2
  100.6 7.5 %fusion.131 = bf16[512,64]{0,1:T(8,128)(2,1)S(1)} fusion(bf16[1,1,20,512,512]{4,3,2,1,0:T(8,128)(2,1)} %param.9, bf16[20,512,64]{1,2,0:T(8,128)(2,1)S(1)} %gather_fusion, pred[20]{0:T(512)(128)(4,1)S(1)} %iota_compare_fusion, bf16[1,1,512,512]{3,2,1,0:T(8,128)(2,1)S(1)} %copy-done, bf16[1,512,64]{1,2,0:T(8,128)(2,1)S(1)} %copy-done.1), kind=kOutput, calls=%fused_computation.47 | convolution fusion | flops 705429504 | bytes 12451860 | tf_op jit(solution)/shard_map/dot_general | solution.py:28
  108.1 1.3 collective-permute-start.1
  109.4 3.7 collective-permute-done.1
  113.1 0.0 copy-done.2
  113.1 0.6 broadcast_select_fusion.2
  113.8 0.0 all-gather.7.cloned.1.call-update
  113.8 0.0 all-gather.9.cloned.1.call-start
  113.9 76.7 %all-gather.7.cloned.1.call-done = bf16[32768,64]{0,1:T(8,128)(2,1)} async-done(((bf16[512,64]{0,1:T(8,128)(2,1)}), bf16[32768,64]{0,1:T(8,128)(2,1)}) %all-gather.7.cloned.1.call-update) | async-done | bytes 4194320 | tf_op jit(solution)/shard_map/all_gather | solution.py:19
  190.6 4.8 %copy.21 = bf16[8,64,8,512]{3,2,0,1:T(8,128)(2,1)} copy(bf16[8,64,8,512]{3,2,1,0:T(8,128)(2,1)} %bitcast.177) | data formatting | bytes 8388608 | tf_op jit(solution)/shard_map/reshape | solution.py:21
  195.3 2.8 gather_fusion.1
  198.2 7.4 %fusion.126 = bf16[512,64]{0,1:T(8,128)(2,1)S(1)} fusion(bf16[1,1,20,512,512]{4,3,2,1,0:T(8,128)(2,1)} %param.9, bf16[20,512,64]{1,2,0:T(8,128)(2,1)S(1)} %gather_fusion.1, pred[20]{0:T(512)(128)(4,1)S(1)} %iota_compare_fusion, bf16[1,1,512,512]{3,2,1,0:T(8,128)(2,1)S(1)} %copy-done, bf16[1,512,64]{1,2,0:T(8,128)(2,1)S(1)} %copy-done.1), kind=kOutput, calls=%fused_computation.46 | convolution fusion | flops 705429504 | bytes 12451860 | tf_op jit(solution)/shard_map/dot_general | solution.py:28
  205.6 1.3 collective-permute-start.2
  206.9 3.7 collective-permute-done.2
  210.6 0.6 broadcast_select_fusion.1
  211.3 0.0 all-gather.9.cloned.1.call-update
  211.3 0.0 all-gather.11.cloned.1.call-start
  211.4 76.7 %all-gather.9.cloned.1.call-done = bf16[32768,64]{0,1:T(8,128)(2,1)} async-done(((bf16[512,64]{0,1:T(8,128)(2,1)}), bf16[32768,64]{0,1:T(8,128)(2,1)}) %all-gather.9.cloned.1.call-update) | async-done | bytes 4194320 | tf_op jit(solution)/shard_map/all_gather | solution.py:19
  288.1 4.8 %copy.20 = bf16[8,64,8,512]{3,2,0,1:T(8,128)(2,1)} copy(bf16[8,64,8,512]{3,2,1,0:T(8,128)(2,1)} %bitcast.178) | data formatting | bytes 8388608 | tf_op jit(solution)/shard_map/reshape | solution.py:21
  292.8 2.8 gather_fusion.2
  295.7 7.4 %fusion.121 = bf16[512,64]{0,1:T(8,128)(2,1)S(1)} fusion(bf16[1,1,20,512,512]{4,3,2,1,0:T(8,128)(2,1)} %param.9, bf16[20,512,64]{1,2,0:T(8,128)(2,1)S(1)} %gather_fusion.2, pred[20]{0:T(512)(128)(4,1)S(1)} %iota_compare_fusion, bf16[1,1,512,512]{3,2,1,0:T(8,128)(2,1)S(1)} %copy-done, bf16[1,512,64]{1,2,0:T(8,128)(2,1)S(1)} %copy-done.1), kind=kOutput, calls=%fused_computation.45 | convolution fusion | flops 705429504 | bytes 12451860 | tf_op jit(solution)/shard_map/dot_general | solution.py:28
  303.1 1.3 collective-permute-start.3
  304.4 3.7 collective-permute-done.3
  308.1 0.6 broadcast_select_fusion
  308.8 0.0 all-gather.11.cloned.1.call-update
  308.8 76.7 %all-gather.11.cloned.1.call-done = bf16[32768,64]{0,1:T(8,128)(2,1)} async-done(((bf16[512,64]{0,1:T(8,128)(2,1)}), bf16[32768,64]{0,1:T(8,128)(2,1)}) %all-gather.11.cloned.1.call-update) | async-done | bytes 4194320 | tf_op jit(solution)/shard_map/all_gather | solution.py:19
  385.6 4.8 %copy.19 = bf16[8,64,8,512]{3,2,0,1:T(8,128)(2,1)} copy(bf16[8,64,8,512]{3,2,1,0:T(8,128)(2,1)} %bitcast.179) | data formatting | bytes 8388608 | tf_op jit(solution)/shard_map/reshape | solution.py:21
  390.3 2.8 gather_fusion.3
  393.2 8.1 %fusion.116 = bf16[1,512,64]{1,2,0:T(8,128)(2,1)} fusion(bf16[1,1,20,512,512]{4,3,2,1,0:T(8,128)(2,1)} %param.9, bf16[20,512,64]{1,2,0:T(8,128)(2,1)S(1)} %gather_fusion.3, pred[20]{0:T(512)(128)(4,1)S(1)} %iota_compare_fusion, bf16[1,1,512,512]{3,2,1,0:T(8,128)(2,1)S(1)} %copy-done, bf16[1,512,64]{1,2,0:T(8,128)(2,1)S(1)} %copy-done.1), kind=kOutput, calls=%fused_computation.44 | convolution fusion | flops 705429504 | bytes 12451860 | tf_op jit(solution)/shard_map/dot_general | solution.py:28
  (3 shorter events, 0.0 us)
Async XLA Ops:
  6.5 94.1 %copy-start = (bf16[1,1,512,512]{3,2,1,0:T(8,128)(2,1)S(1)}, bf16[1,1,512,512]{3,2,1,0:T(8,128)(2,1)}, u32[]{:S(2)}) copy-start(bf16[1,1,512,512]{3,2,1,0:T(8,128)(2,1)} %param.8) | copy-start | bytes 1572868
  6.5 86.4 %all-gather.5.cloned.1.call-start = ((), (), s32[]{:S(2)}) async-start(), calls=%async_computation | async-start | bytes 4259840 | tf_op jit(solution)/shard_map/all_gather | solution.py:19
  6.5 5.1 %collective-permute-start = (bf16[512,64]{0,1:T(8,128)(2,1)S(1)}, bf16[512,64]{0,1:T(8,128)(2,1)S(1)}, u32[]{:S(2)}, u32[]{:S(2)}) collective-permute-start(bf16[512,64]{0,1:T(8,128)(2,1)S(1)} %broadcast_in_dim.39), channel_id=1, source_target_pairs={{0,64},{64,128},{128,192},{1,65},{65,129},{129,193},{2,66},{66,130... | collective-permute-start | bytes 196616 | tf_op jit(solution)/shard_map/ppermute | solution.py:12
  12.4 178.2 %all-gather.7.cloned.1.call-start = ((), (), s32[]{:S(2)}) async-start(), calls=%async_computation.1 | async-start | bytes 4259840 | tf_op jit(solution)/shard_map/all_gather | solution.py:19
  97.8 2.9 copy-start.1
  100.6 12.5 %copy-start.2 = (bf16[512,64]{0,1:T(8,128)(2,1)S(1)}, bf16[512,64]{0,1:T(8,128)(2,1)}, u32[]{:S(2)}) copy-start(bf16[512,64]{0,1:T(8,128)(2,1)} %param.7) | copy-start | bytes 196612
  108.1 5.0 %collective-permute-start.1 = (bf16[512,64]{0,1:T(8,128)(2,1)S(1)}, bf16[512,64]{0,1:T(8,128)(2,1)S(1)}, u32[]{:S(2)}, u32[]{:S(2)}) collective-permute-start(bf16[512,64]{0,1:T(8,128)(2,1)S(1)} %fusion.131), channel_id=1, source_target_pairs={{0,64},{64,128},{128,192},{1,65},{65,129},{129,193},{2,66},{66,130... | collective-permute-start | bytes 196616 | tf_op jit(solution)/shard_map/ppermute | solution.py:12
  113.8 174.2 %all-gather.9.cloned.1.call-start = ((), (), s32[]{:S(2)}) async-start(), calls=%async_computation.2 | async-start | bytes 4259840 | tf_op jit(solution)/shard_map/all_gather | solution.py:19
  205.6 5.0 %collective-permute-start.2 = (bf16[512,64]{0,1:T(8,128)(2,1)S(1)}, bf16[512,64]{0,1:T(8,128)(2,1)S(1)}, u32[]{:S(2)}, u32[]{:S(2)}) collective-permute-start(bf16[512,64]{0,1:T(8,128)(2,1)S(1)} %fusion.126), channel_id=1, source_target_pairs={{0,64},{64,128},{128,192},{1,65},{65,129},{129,193},{2,66},{66,130... | collective-permute-start | bytes 196616 | tf_op jit(solution)/shard_map/ppermute | solution.py:12
  211.3 174.2 %all-gather.11.cloned.1.call-start = ((), (), s32[]{:S(2)}) async-start(), calls=%async_computation.3 | async-start | bytes 4259840 | tf_op jit(solution)/shard_map/all_gather | solution.py:19
  303.1 5.0 %collective-permute-start.3 = (bf16[512,64]{0,1:T(8,128)(2,1)S(1)}, bf16[512,64]{0,1:T(8,128)(2,1)S(1)}, u32[]{:S(2)}, u32[]{:S(2)}) collective-permute-start(bf16[512,64]{0,1:T(8,128)(2,1)S(1)} %fusion.121), channel_id=1, source_target_pairs={{0,64},{64,128},{128,192},{1,65},{65,129},{129,193},{2,66},{66,130... | collective-permute-start | bytes 196616 | tf_op jit(solution)/shard_map/ppermute | solution.py:12
Sparse Core Ops, SparseCore 0:
  12.5 80.4 all-gather.4
  113.9 76.5 all-gather.6
  211.4 76.5 all-gather.8
  308.9 76.5 all-gather.10
where the time goes:
time: 409 us; the launch traced here: 408 us
  waiting for transfers between devices  324 us (79%)
  local copies, waits for them, and re-layouts  30.5 us (7%)
  matrix products  30.5 us (7%)
  between operations  13.9 us (3%)
  starting transfers between devices  5.43 us (1%)
    all_gather x4, waiting for transfers between devices, advance(): gathered = lax.all_gather(incoming, 'row', axis=0, tiled=True)  309 us
    dot_general x4, matrix products, advance(): jnp.dot(solve_row, coupled, preferred_element_type=jnp.float32)  30.5 us
    reshape x4, local copies, waits for them, and re-layouts, advance(): tiles = gathered.reshape(-1, TILE, width)  19.2 us
    ppermute x4, waiting for transfers between devices, shifted(): return lax.ppermute(array, axis, pairs)  14.8 us
    gather x4, local copies, waits for them, and re-layouts, advance(): chosen = tiles[cols_row]  11.3 us
  transfers between devices with their start and end apart: 8, of which 8 were waited for; matrix products, arithmetic and copies ran while one was open for 0% of the time, Pallas kernels for 0%

commit v1 on v0

v1 whole, which is shorter than its diff:
```python
import functools

import jax
import jax.numpy as jnp
from jax import lax
from jax.experimental import pallas as pl
from jax.experimental.pallas import tpu as pltpu
from jax.sharding import PartitionSpec as P

MESH = pl.DeviceIdType.MESH
NY = 4
CHUNKS = 2
SEGS = 5


def offsets(nz):
    order = [0]
    for d in range(nz // 2, 0, -1):
        order.append(d)
        if d != nz - d:
            order.append(nz - d)
    return order


def nt(a, b):
    return lax.dot_general(a, b, (((1,), (1,)), ((), ())), preferred_element_type=jnp.float32)


def kernel(ns, nz, cols_ref, count_ref, inflow_ref, forcing_ref, solve_hbm, greens_hbm, out_ref,
           *scratch):
    held = scratch[:CHUNKS]
    (sent, greens, solve, acc, local_sem, a_recv, b_recv, r_recv, d_recv, send_sem) = scratch[CHUNKS:]
    chunks, rows = CHUNKS, sent.shape[1]
    kmax = greens.shape[0]
    ny = NY
    s = lax.axis_index("slab")
    r = lax.axis_index("row")
    y, z, c = r // (2 * nz), (r // 2) % nz, r % 2
    up, down = (s + 1) % ns, (s + ns - 1) % ns
    yp, ym, y2 = (y + 1) % ny, (y + ny - 1) % ny, (y + 2) % ny
    order = offsets(nz)

    def at(slab, yy, zz, cc):
        return (slab, yy * (2 * nz) + zz * 2 + cc)

    g_copy = pltpu.make_async_copy(greens_hbm, greens, local_sem.at[0])
    s_copy = pltpu.make_async_copy(solve_hbm, solve, local_sem.at[1])
    g_copy.start()
    s_copy.start()

    barrier = pltpu.get_barrier_semaphore()
    for d in order:
        pl.semaphore_signal(barrier, 1, device_id=at(down, y, (z + d) % nz, c), device_id_type=MESH)
    for peer in (at(s, yp, z, c), at(s, ym, z, c), at(s, y, z, 1 - c)):
        pl.semaphore_signal(barrier, 1, device_id=peer, device_id_type=MESH)
    pl.semaphore_wait(barrier, nz + 3)

    def remote(src, dst, ssem, rsem, peer):
        return pltpu.make_async_remote_copy(
            src_ref=src, dst_ref=dst, send_sem=ssem, recv_sem=rsem, device_id=peer, device_id_type=MESH
        )

    def tile(ch, cc, yy, zz):
        return held[ch].at[cc, yy * nz + zz]

    def group(ch, cc, yy):
        return held[ch].at[cc, pl.ds(yy * nz, nz)]

    def launch(src, ch):
        for p, d in enumerate(order):
            remote(src, tile(ch, c, y, z), send_sem.at[ch, 0], a_recv.at[ch, p],
                   at(up, y, (z + d) % nz, c)).start()

    def step_a(ch, p):
        zz = (z + nz - order[p]) % nz
        t = tile(ch, c, y, zz)
        pltpu.make_async_copy(t, t, a_recv.at[ch, p]).wait()
        remote(t, t, send_sem.at[ch, 1], b_recv.at[ch, 0, p], at(s, yp, z, c)).start()
        remote(t, t, send_sem.at[ch, 1], b_recv.at[ch, 1, p], at(s, ym, z, c)).start()

    def share(ch, yy, i):
        t = group(ch, c, yy)
        remote(t, t, send_sem.at[ch, 3], d_recv.at[ch, i], at(s, y, z, 1 - c)).start()

    def step_b(ch, p):
        zz = (z + nz - order[p]) % nz
        tp, tm = tile(ch, c, ym, zz), tile(ch, c, yp, zz)
        pltpu.make_async_copy(tp, tp, b_recv.at[ch, 0, p]).wait()
        if p % 2 == 0:
            remote(tp, tp, send_sem.at[ch, 2], r_recv.at[ch], at(s, yp, z, c)).start()
        pltpu.make_async_copy(tm, tm, b_recv.at[ch, 1, p]).wait()
        if p % 2 == 1:
            remote(tm, tm, send_sem.at[ch, 2], r_recv.at[ch], at(s, ym, z, c)).start()

    def gather_tail(ch):
        share(ch, y, 0)
        for p in range(nz):
            step_b(ch, p)
        share(ch, ym, 1)
        share(ch, yp, 2)
        g = group(ch, c, y2)
        pltpu.make_async_copy(g, g, r_recv.at[ch]).wait()
        share(ch, y2, 3)
        for i, yy in enumerate((y, ym, yp, y2)):
            g = group(ch, 1 - c, yy)
            pltpu.make_async_copy(g, g, d_recv.at[ch, i]).wait()

    count = count_ref[0]

    def slot(ch, k):
        j = cols_ref[k]
        zlow = jnp.bitwise_and(lax.shift_right_logical(j, 1), nz - 1)
        yhigh = lax.div(j, jnp.int32(2 * nz))
        x = held[ch][jnp.bitwise_and(j, 1), yhigh * nz + zlow]
        x = jnp.where(k < count, x, jnp.zeros_like(x))
        return nt(x, greens[k])

    @pl.when(s == ns - 1)
    def _():
        for ch in range(chunks):
            launch(inflow_ref.at[pl.ds(ch * rows, rows)], ch)

    for p in range(nz):
        step_a(0, p)
    per = kmax // SEGS
    for ch in range(chunks):
        gather_tail(ch)
        if ch == 0:
            g_copy.wait()
            s_copy.wait()
        pending = list(range(nz)) if ch + 1 < chunks else []
        each = -(-nz // (SEGS - 1))
        for seg in range(SEGS):
            total = slot(ch, seg * per)
            for k in range(1, per):
                total += slot(ch, seg * per + k)
            if seg == 0:
                acc[...] = total + forcing_ref[pl.ds(ch * rows, rows)].astype(jnp.float32)
            elif seg < SEGS - 1:
                acc[...] += total
            for p in pending[:each]:
                step_a(ch + 1, p)
            pending = pending[each:]
        coupled = (acc[...] + total).astype(jnp.bfloat16)
        result = nt(coupled, solve[...]).astype(jnp.bfloat16)
        sent[ch] = result
        out_ref[pl.ds(ch * rows, rows)] = result

        @pl.when(s < ns - 1)
        def _():
            launch(sent.at[ch], ch)

    for ch in range(chunks):
        for i, (n, w) in enumerate(((nz, 0), (2 * nz, 0), (nz, 0), (ny * nz, 0))):
            g = held[ch].at[w, pl.ds(0, n)]
            pltpu.make_async_copy(g, g, send_sem.at[ch, i]).wait()


def shards(ns, nrow, forcing, inflow, self_solve, greens, kept_cols, counts):
    nz = nrow // (2 * NY)
    tile, columns = inflow.shape
    kmax = greens.shape[2]
    rows = columns // CHUNKS
    vmem = pl.BlockSpec(memory_space=pltpu.VMEM)
    smem = pl.BlockSpec(memory_space=pltpu.SMEM)
    hbm = pl.BlockSpec(memory_space=pltpu.HBM)
    dma = pltpu.SemaphoreType.DMA
    out = pl.pallas_call(
        functools.partial(kernel, ns, nz),
        name="sweep",
        out_shape=jax.ShapeDtypeStruct((columns, tile), jnp.bfloat16),
        in_specs=[smem, smem, vmem, vmem, hbm, hbm],
        out_specs=vmem,
        scratch_shapes=[
            *[pltpu.VMEM((2, NY * nz, rows, tile), jnp.bfloat16)] * CHUNKS,
            pltpu.VMEM((CHUNKS, rows, tile), jnp.bfloat16),
            pltpu.VMEM((kmax, tile, tile), jnp.bfloat16),
            pltpu.VMEM((tile, tile), jnp.bfloat16),
            pltpu.VMEM((rows, tile), jnp.float32),
            dma((2,)),
            dma((CHUNKS, nz)),
            dma((CHUNKS, 2, nz)),
            dma((CHUNKS,)),
            dma((CHUNKS, 4)),
            dma((CHUNKS, 4)),
        ],
        compiler_params=pltpu.CompilerParams(
            collective_id=0, has_side_effects=True, vmem_limit_bytes=40 * 1024 * 1024
        ),
    )(kept_cols.reshape(kmax), counts.reshape(1), inflow.T, forcing[0].T, self_solve[0, 0], greens[0, 0])
    return out.T[None]


def solution(mesh):
    placed = (
        P("slab", "row", None),
        P("row", None),
        P("slab", "row", None, None),
        P("slab", "row", None, None, None),
        P("slab", "row", None),
        P("slab", "row"),
    )
    return jax.shard_map(
        functools.partial(shards, mesh.shape["slab"], mesh.shape["row"]),
        mesh=mesh, in_specs=placed, out_specs=P("slab", "row", None), check_vma=False,
    )
```

time: 409 us -> 123 us (0.30)
  waiting for transfers between devices: 324 us -> 0 us
  Pallas kernels: 0 us -> 114 us
  matrix products: 30.5 us -> 0 us
  local copies, waits for them, and re-layouts: 30.5 us -> 7.98 us
  between operations: 13.9 us -> 0.67 us
  starting transfers between devices: 5.43 us -> 0 us
    all_gather x4 -> x0, waiting for transfers between devices: 309 us -> none  [advance(): gathered = lax.all_gather(incoming, 'row', axis=0, tiled=True)]
    pallas_call x0 -> x1, Pallas kernels: none -> 114 us  [shards(): pl.pallas_call(functools.partial(kernel, ns, nz), name='sweep', out_shape...]
    dot_general x4 -> x0, matrix products: 30.5 us -> none  [advance(): jnp.dot(solve_row, coupled, preferred_element_type=jnp.float32)]
    reshape x4 -> x0, local copies, waits for them, and re-layouts: 19.2 us -> none  [advance(): tiles = gathered.reshape(-1, TILE, width)]
    ppermute x4 -> x0, waiting for transfers between devices: 14.8 us -> none  [shifted(): return lax.ppermute(array, axis, pairs)]
    gather x4 -> x0, local copies, waits for them, and re-layouts: 11.3 us -> none  [advance(): chosen = tiles[cols_row]]
    unnamed x6 -> x11, local copies, waits for them, and re-layouts: 0.01 us -> 7.98 us
    ppermute x4 -> x0, starting transfers between devices: 5.3 us -> none  [shifted(): return lax.ppermute(array, axis, pairs)]
  transfers between devices with their start and end apart: 8 -> 0, of which waited for: 8 -> 0; matrix products, arithmetic and copies ran while one was open for 0% -> 0% of each run, Pallas kernels for 0% -> 0%
where the time goes in v1:
time: 123 us
  Pallas kernels  114 us (93%)
  local copies, waits for them, and re-layouts  7.98 us (6%)
    pallas_call x1, Pallas kernels, shards(): pl.pallas_call(functools.partial(kernel, ns, nz), name='sweep', out_shape...  114 us
    unnamed x11, local copies, waits for them, and re-layouts  7.98 us

profile of v1, /device:TPU:7, one launch (start us, length us, event | category | flops | bytes accessed | tf_op | source)
XLA Modules:
  0.0 122.7 jit_solution(3598976098857998364)
XLA Ops:
  0.7 0.0 copy-start
  0.7 4.0 %copy-done = bf16[1,1,20,512,512]{4,3,2,1,0:T(8,128)(2,1)S(1)} copy-done((bf16[1,1,20,512,512]{4,3,2,1,0:T(8,128)(2,1)S(1)}, bf16[1,1,20,512,512]{4,3,2,1,0:T(8,128)(2,1)}, u32[]{:S(2)}) %copy-start) | copy-done | bytes 10485784
  4.6 0.0 copy-start.1
  4.6 1.0 copy-done.1
  5.7 0.0 copy-start.2
  5.7 0.8 copy-done.2
  6.5 0.0 copy-start.3
  6.5 0.8 copy-done.3
  7.4 0.0 copy-start.4
  7.4 0.7 copy-done.4
  8.0 114.0 %sweep.1 = bf16[64,512]{1,0:T(8,128)(2,1)S(1)} custom-call(s32[20]{0:T(128)S(1)} %bitcast.17, s32[1]{0:T(128)} %bitcast.11.count_ref, bf16[64,512]{1,0:T(8,128)(2,1)S(1)} %bitcast.15, bf16[64,512]{1,0:T(8,128)(2,1)S(1)} %bitcast.16, bf16[512,512]{1,0:T(8,128)(2,1)S(1)} %bitcast.13, bf16[20,512,512]{2,1,0:T(8,128)(2,1)S(1)} %bitcast.12), custom_call_target="tpu_custom_call" | custom-call | tf_op jit(solution)/shard_map/sweep/pallas_call | solution.py:168
  122.0 0.6 copy.9
Async XLA Ops:
  0.7 4.0 %copy-start = (bf16[1,1,20,512,512]{4,3,2,1,0:T(8,128)(2,1)S(1)}, bf16[1,1,20,512,512]{4,3,2,1,0:T(8,128)(2,1)}, u32[]{:S(2)}) copy-start(bf16[1,1,20,512,512]{4,3,2,1,0:T(8,128)(2,1)} %param.9) | copy-start | bytes 31457284
  4.6 1.0 copy-start.1
  5.7 0.8 copy-start.2
  6.5 0.8 copy-start.3
  7.4 0.7 copy-start.4

commit v2 on v0

v2 whole, which is shorter than its diff:
```python
import functools
import jax
import jax.numpy as jnp
from jax import lax
from jax.experimental import pallas as pl
from jax.experimental.pallas import tpu as pltpu
from jax.sharding import PartitionSpec as P

MESH = pl.DeviceIdType.MESH
NY = 4

def offsets(nz):
    order = []
    for d in range(nz // 2, 0, -1):
        order.append(d)
        if d != nz - d:
            order.append(nz - d)
    return order + [0]

def nt(a, b):
    return lax.dot_general(a, b, (((1,), (1,)), ((), ())), preferred_element_type=jnp.float32)

C = 8
F = {'seq': 'AFB', 'lb': 1, 'lf': 2, 'G': 2, 'D': True, 'M': True}


def kernel(ns, nz, cols_ref, count_ref, inflow_hbm, forcing_hbm, solve_hbm, greens_hbm, out_ref, *scratch):
    held = scratch[:C]
    (sent, result, inflow, packed, forcing, greens, turned, solve, solve_t, table, local_sem, g_sem, a_recv, b_recv, d_recv, send_sem) = scratch[C:]
    rows, depth = sent.shape[1:]
    pack = greens.shape[1] // depth
    width = rows // pack
    kmax = greens.shape[0]
    ny = NY
    G = F.get('G', 2)
    s = lax.axis_index("slab")
    r = lax.axis_index("row")
    y, z, c = r // (2 * nz), (r // 2) % nz, r % 2
    up, down = (s + 1) % ns, (s + ns - 1) % ns
    ys = [(y + j) % ny for j in range(ny)]
    order = offsets(nz)
    JS = (2, 1, 3)

    def at(slab, yy, zz, cc):
        return (slab, yy * (2 * nz) + zz * 2 + cc)

    i_copy = pltpu.make_async_copy(inflow_hbm, inflow, local_sem.at[0])
    s_copy = pltpu.make_async_copy(solve_hbm, solve, local_sem.at[1])
    def g_copy(k):
        return pltpu.make_async_copy(greens_hbm.at[k], greens.at[k], g_sem.at[k])
    f_copy = pltpu.make_async_copy(forcing_hbm, forcing, local_sem.at[2])
    i_copy.start()
    f_copy.start()
    s_copy.start()
    for k in range(kmax):
        g_copy(k).start()

    def piece(ref, ch):
        lo = ch * width // rows * rows
        block = ref[pl.ds(lo, rows)].astype(jnp.float32)
        return block[ch * width - lo:ch * width - lo + width]

    def fold(v):
        return jnp.concatenate([v[:, h * depth:(h + 1) * depth] for h in range(pack)], axis=0).astype(jnp.bfloat16)

    barrier = pltpu.get_barrier_semaphore()
    for d in order:
        pl.semaphore_signal(barrier, 1, device_id=at(down, y, (z + d) % nz, c), device_id_type=MESH)
    for j in JS:
        pl.semaphore_signal(barrier, 1, device_id=at(s, ys[j], z, c), device_id_type=MESH)
    pl.semaphore_signal(barrier, 1, device_id=at(s, y, z, 1 - c), device_id_type=MESH)

    for k in range(kmax):
        j = cols_ref[k]
        d = jnp.bitwise_and(z - lax.shift_right_logical(j, 1), nz - 1)
        p = jnp.int32(0)
        for i, o in enumerate(order):
            if i: p = jnp.where(d == o, jnp.int32(i), p)
        table[k] = jnp.bitwise_and(j, 1) * (ny * nz) + lax.div(j, jnp.int32(2 * nz)) * nz + p
    i_copy.wait()
    for ch in range(C):
        packed[ch] = fold(piece(inflow, ch))
    pl.semaphore_wait(barrier, nz + 4)

    def remote(src, dst, ssem, rsem, peer):
        return pltpu.make_async_remote_copy(src_ref=src, dst_ref=dst, send_sem=ssem, recv_sem=rsem, device_id=peer, device_id_type=MESH)

    def block(ch, cc, yy, p, n=1):
        return held[ch].at[pl.ds(cc * (ny * nz) + yy * nz + p, n)]

    def launch(src, ch):
        for p, d in enumerate(order):
            remote(src, block(ch, c, y, p), send_sem.at[ch, 0], a_recv.at[ch, p], at(up, y, (z + d) % nz, c)).start()

    def done(t, sem):
        pltpu.make_async_copy(t, t, sem).wait()

    per_g = nz // G
    def step_a(ch, p):
        t = block(ch, c, y, p)
        done(t, a_recv.at[ch, p])
        for j in JS:
            remote(t, t, send_sem.at[ch, 1], b_recv.at[ch, j - 1, p // per_g], at(s, ys[j], z, c)).start()
        if p % per_g == per_g - 1 and F['D']:
            g = block(ch, c, y, p - per_g + 1, per_g)
            remote(g, g, send_sem.at[ch, 2], d_recv.at[ch, 0, p // per_g], at(s, y, z, 1 - c)).start()

    def step_b(ch, q):
        for j in (1, 3, 2):
            g = block(ch, c, ys[j], q * per_g, per_g)
            done(g, b_recv.at[ch, (ny - j) % ny - 1, q])
            if F['D']:
                remote(g, g, send_sem.at[ch, 2], d_recv.at[ch, j, q], at(s, y, z, 1 - c)).start()

    def finish(ch):
        if F['D']:
            for q in range(G):
                for j in (0, 1, 3, 2):
                    g = block(ch, 1 - c, ys[j], q * per_g, per_g)
                    done(g, d_recv.at[ch, j, q])

    count = count_ref[0]

    def compute(ch):
        totals = [jnp.zeros((rows, turned.shape[2]), jnp.float32)] * pack
        for k in range(kmax):
            x = held[ch][table[k]]
            x = jnp.where(k < count, x, jnp.zeros_like(x))
            for h in range(pack):
                totals[h] += jnp.dot(x, turned[k, pl.ds(h * depth, depth)], preferred_element_type=jnp.float32)
        v = piece(forcing, ch)
        for h in range(pack):
            v += totals[h][h * width:(h + 1) * width]
        v = jnp.dot(v.astype(jnp.bfloat16), solve_t[...], preferred_element_type=jnp.float32)
        sent[ch] = fold(v)

        @pl.when(s < ns - 1)
        def _():
            launch(sent.at[pl.ds(ch, 1)], ch)
        result[pl.ds(ch * width, width)] = v

    @pl.when(s == ns - 1)
    def _():
        for ch in range(C):
            launch(packed.at[pl.ds(ch, 1)], ch)

    def turn(k, carry):
        g_copy(k).wait()
        turned[k] = greens[k].T
        return carry
    lax.fori_loop(0, kmax, turn, 0)
    s_copy.wait()
    solve_t[...] = solve[...].T
    f_copy.wait()

    lb, lf = F['lb'], F['lf']
    for t in range(C + lf):
        for e in F['seq']:
            if e == 'A' and t < C:
                for p in range(nz):
                    step_a(t, p)
            if e == 'B' and 0 <= t - lb < C:
                for q in range(G):
                    step_b(t - lb, q)
            if e == 'F' and 0 <= t - lf < C:
                finish(t - lf)
                compute(t - lf)
    out_ref[...] = result[...].astype(jnp.bfloat16)

    for ch in range(C):
        for i, n in enumerate((nz, 3 * nz, ny * nz)):
            if i == 2 and not F['D']: continue
            g = held[ch].at[pl.ds(0, n)]
            done(g, send_sem.at[ch, i])

def shards(ns, nrow, forcing, inflow, self_solve, greens, kept_cols, counts):
    nz = nrow // (2 * NY)
    tile, columns = inflow.shape
    kmax = greens.shape[2]
    rows = 16
    depth = tile * columns // (C * rows)
    vmem = pl.BlockSpec(memory_space=pltpu.VMEM)
    smem = pl.BlockSpec(memory_space=pltpu.SMEM)
    hbm = pl.BlockSpec(memory_space=pltpu.HBM)
    dma = pltpu.SemaphoreType.DMA
    G = F.get('G', 2)
    out = pl.pallas_call(
        functools.partial(kernel, ns, nz), name="sweep",
        out_shape=jax.ShapeDtypeStruct((columns, tile), jnp.bfloat16),
        in_specs=[smem, smem, hbm, hbm, hbm, hbm], out_specs=vmem,
        scratch_shapes=[
            *[pltpu.VMEM((2 * NY * nz, rows, depth), jnp.bfloat16)] * C,
            pltpu.VMEM((C, rows, depth), jnp.bfloat16),
            pltpu.VMEM((columns, tile), jnp.float32),
            pltpu.VMEM((columns, tile), jnp.bfloat16),
            pltpu.VMEM((C, rows, depth), jnp.bfloat16),
            pltpu.VMEM((columns, tile), jnp.bfloat16),
            pltpu.VMEM((kmax, tile, tile), jnp.bfloat16),
            pltpu.VMEM((kmax, tile, tile), jnp.bfloat16),
            pltpu.VMEM((tile, tile), jnp.bfloat16),
            pltpu.VMEM((tile, tile), jnp.bfloat16),
            pltpu.SMEM((kmax,), jnp.int32),
            dma((3,)), dma((kmax,)), dma((C, nz)), dma((C, 3, G)), dma((C, 4, G)), dma((C, 3)),
        ],
        compiler_params=pltpu.CompilerParams(collective_id=0, has_side_effects=True, vmem_limit_bytes=63 * 1024 * 1024),
    )(kept_cols.reshape(kmax), counts.reshape(1), inflow.T, forcing[0].T, self_solve[0, 0], greens[0, 0])
    return out.T[None]


def solution(mesh):
    placed = (
        P("slab", "row", None),
        P("row", None),
        P("slab", "row", None, None),
        P("slab", "row", None, None, None),
        P("slab", "row", None),
        P("slab", "row"),
    )
    return jax.shard_map(
        functools.partial(shards, mesh.shape["slab"], mesh.shape["row"]),
        mesh=mesh, in_specs=placed, out_specs=P("slab", "row", None), check_vma=False,
    )
```

time: 409 us -> 88 us (0.22)
  waiting for transfers between devices: 324 us -> 0 us
  Pallas kernels: 0 us -> 85.7 us
  matrix products: 30.5 us -> 0 us
  local copies, waits for them, and re-layouts: 30.5 us -> 1.47 us
  between operations: 13.9 us -> 0.66 us
  starting transfers between devices: 5.43 us -> 0 us
    all_gather x4 -> x0, waiting for transfers between devices: 309 us -> none  [advance(): gathered = lax.all_gather(incoming, 'row', axis=0, tiled=True)]
    pallas_call x0 -> x1, Pallas kernels: none -> 85.7 us  [shards(): pl.pallas_call(functools.partial(kernel, ns, nz), name='sweep', out_shape...]
    dot_general x4 -> x0, matrix products: 30.5 us -> none  [advance(): jnp.dot(solve_row, coupled, preferred_element_type=jnp.float32)]
    reshape x4 -> x0, local copies, waits for them, and re-layouts: 19.2 us -> none  [advance(): tiles = gathered.reshape(-1, TILE, width)]
    ppermute x4 -> x0, waiting for transfers between devices: 14.8 us -> none  [shifted(): return lax.ppermute(array, axis, pairs)]
    gather x4 -> x0, local copies, waits for them, and re-layouts: 11.3 us -> none  [advance(): chosen = tiles[cols_row]]
    ppermute x4 -> x0, starting transfers between devices: 5.3 us -> none  [shifted(): return lax.ppermute(array, axis, pairs)]
  transfers between devices with their start and end apart: 8 -> 0, of which waited for: 8 -> 0; matrix products, arithmetic and copies ran while one was open for 0% -> 0% of each run, Pallas kernels for 0% -> 0%
where the time goes in v2:
time: 88 us; the launch traced here: 87.8 us
  Pallas kernels  85.7 us (97%)
  local copies, waits for them, and re-layouts  1.47 us (2%)
    pallas_call x1, Pallas kernels, shards(): pl.pallas_call(functools.partial(kernel, ns, nz), name='sweep', out_shape...  85.7 us

profile of v2, /device:TPU:7, one launch (start us, length us, event | category | flops | bytes accessed | tf_op | source)
XLA Modules:
  0.0 87.8 jit_solution(9587370721700806428)
XLA Ops:
  0.7 85.7 %sweep.1 = bf16[64,512]{1,0:T(8,128)(2,1)} custom-call(s32[20]{0:T(128)} %bitcast.17, s32[1]{0:T(128)} %bitcast.11.count_ref, bf16[64,512]{1,0:T(8,128)(2,1)} %bitcast.15, bf16[64,512]{1,0:T(8,128)(2,1)} %bitcast.16, bf16[512,512]{1,0:T(8,128)(2,1)} %bitcast.13, bf16[20,512,512]{2,1,0:T(8,128)(2,1)} %bitcast.12), custom_call_target="tpu_custom_call" | custom-call | tf_op jit(solution)/shard_map/sweep/pallas_call | solution.py:187
  86.4 1.5 %copy.9 = bf16[1,512,64]{1,2,0:T(8,128)(2,1)} copy(bf16[1,512,64]{1,2,0:T(8,128)(2,1)} %bitcast.14) | data formatting | bytes 131072

commit v3 on v0

v3 whole, which is shorter than its diff:
```python
import functools

import jax
import jax.numpy as jnp
from jax import lax
from jax.experimental import pallas as pl
from jax.experimental.pallas import tpu as pltpu
from jax.sharding import PartitionSpec as P

MESH = pl.DeviceIdType.MESH
NY = 4
ROWS = 16
GROUPS = 1
HOPS = (2, 1, 3)
WIDTHS = (8,) * 8


def offsets(nz):
    order = [0]
    for d in range(1, nz // 2 + 1):
        order.append(d)
        if d != nz - d:
            order.append(nz - d)
    return order


def kernel(widths, ns, nz, cols_ref, count_ref, inflow_hbm, forcing_hbm, solve_hbm, greens_hbm, out_ref, *scratch):
    C = len(widths)
    starts = [sum(widths[:i]) for i in range(C)]
    held, sent, packed = scratch[:C], scratch[C:2 * C], scratch[2 * C:3 * C]
    (inflow, forcing, greens, turned, solve, solve_t, table,
     local_sem, g_sem, a_recv, b_recv, d_recv, send_sem) = scratch[3 * C:]
    tile, kmax, ny = greens.shape[1], greens.shape[0], NY
    s = lax.axis_index("slab")
    r = lax.axis_index("row")
    y, z, c = r // (2 * nz), (r // 2) % nz, r % 2
    ys = [(y + j) % ny for j in range(ny)]
    order = offsets(nz)
    per_g = nz // GROUPS

    def at(slab, yy, zz, cc):
        return (slab, yy * (2 * nz) + zz * 2 + cc)

    own = order.index(0)
    barrier = pltpu.get_barrier_semaphore()

    def greet(*place):
        pl.semaphore_signal(barrier, 1, device_id=at(*place), device_id_type=MESH)

    @pl.when(s == 0)
    def _():
        for d in order:
            if d:
                greet(s, y, (z + d) % nz, c)

    @pl.when(s > 0)
    def _():
        for d in order:
            greet(s - 1, y, (z + d) % nz, c)

    for j in HOPS:
        greet(s, ys[j], z, c)
    greet(s, y, z, 1 - c)

    def g_copy(k):
        return pltpu.make_async_copy(greens_hbm.at[k], greens.at[k], g_sem.at[k])

    i_copy = pltpu.make_async_copy(inflow_hbm, inflow, local_sem.at[0])
    s_copy = pltpu.make_async_copy(solve_hbm, solve, local_sem.at[1])
    f_copy = pltpu.make_async_copy(forcing_hbm, forcing, local_sem.at[2])
    i_copy.start()
    f_copy.start()
    s_copy.start()
    for k in range(kmax):
        g_copy(k).start()

    def piece(ref, ch):
        lo = starts[ch] // ROWS * ROWS
        hi = -(-(starts[ch] + widths[ch]) // ROWS) * ROWS
        block = ref[pl.ds(lo, hi - lo)].astype(jnp.float32)
        return block[starts[ch] - lo:starts[ch] - lo + widths[ch]]

    def fold(v, ch):
        depth = tile * widths[ch] // ROWS
        pieces = [v[:, h * depth:(h + 1) * depth] for h in range(tile // depth)]
        return (jnp.concatenate(pieces, axis=0) if len(pieces) > 1 else v).astype(jnp.bfloat16)

    i_copy.wait()
    for ch in range(C):
        packed[ch][0] = fold(piece(inflow, ch), ch)
    for k in range(kmax):
        j = cols_ref[k]
        d = jnp.bitwise_and(z - lax.shift_right_logical(j, 1), nz - 1)
        p = jnp.int32(0)
        for i, o in enumerate(order):
            p = jnp.where(d == o, jnp.int32(i), p)
        table[k] = jnp.bitwise_and(j, 1) * (ny * nz) + lax.div(j, jnp.int32(2 * nz)) * nz + p

    @pl.when(s == 0)
    def _():
        pl.semaphore_wait(barrier, 2 * nz + 3)

    @pl.when(jnp.logical_and(s > 0, s < ns - 1))
    def _():
        pl.semaphore_wait(barrier, nz + 4)

    @pl.when(s == ns - 1)
    def _():
        pl.semaphore_wait(barrier, 4)

    def remote(src, dst, ssem, rsem, peer):
        return pltpu.make_async_remote_copy(
            src_ref=src, dst_ref=dst, send_sem=ssem, recv_sem=rsem, device_id=peer, device_id_type=MESH
        )

    def done(t, sem):
        pltpu.make_async_copy(t, t, sem).wait()

    def block(ch, cc, yy, p, n=1):
        return held[ch].at[pl.ds(cc * (ny * nz) + yy * nz + p, n)]

    def launch(src, ch):
        for p, d in enumerate(order):
            remote(src, block(ch, c, y, p), send_sem.at[ch, 0], a_recv.at[ch, p], at(s + 1, y, (z + d) % nz, c)).start()

    def share(ch, j, q):
        g = block(ch, c, ys[j], q * per_g, per_g)
        remote(g, g, send_sem.at[ch, 2], d_recv.at[ch, j, q], at(s, y, z, 1 - c)).start()

    def stage_a(ch):
        for p in range(nz):
            t = block(ch, c, y, p)
            if p == own:
                @pl.when(s > 0)
                def _():
                    done(t, a_recv.at[ch, p])
            else:
                done(t, a_recv.at[ch, p])
            for j in HOPS:
                remote(t, t, send_sem.at[ch, 1], b_recv.at[ch, j - 1, p // per_g], at(s, ys[j], z, c)).start()
            if p % per_g == per_g - 1:
                share(ch, 0, p // per_g)

    def stage_b(ch):
        for q in range(GROUPS):
            for j in (1, 3, 2):
                done(block(ch, c, ys[j], q * per_g, per_g), b_recv.at[ch, (ny - j) % ny - 1, q])
                share(ch, j, q)

    count = count_ref[0]

    def arrive(ch):
        for q in range(GROUPS):
            for j in (0, 1, 3, 2):
                done(block(ch, 1 - c, ys[j], q * per_g, per_g), d_recv.at[ch, j, q])

    def finish(ch):
        arrive(ch)
        width, depth = widths[ch], tile * widths[ch] // ROWS
        pack = tile // depth
        totals = [jnp.zeros((ROWS, tile), jnp.float32)] * pack
        for k in range(kmax):
            x = held[ch][table[k]]
            x = jnp.where(k < count, x, jnp.zeros_like(x))
            for h in range(pack):
                totals[h] += jnp.dot(x, turned[k, pl.ds(h * depth, depth)], preferred_element_type=jnp.float32)
        v = piece(forcing, ch)
        for h in range(pack):
            v += totals[h][h * width:(h + 1) * width]
        v = jnp.dot(v.astype(jnp.bfloat16), solve_t[...], preferred_element_type=jnp.float32)
        sent[ch][0] = fold(v, ch)

        @pl.when(s < ns - 1)
        def _():
            launch(sent[ch], ch)
        out_ref[pl.ds(starts[ch], width)] = v

    @pl.when(s == 0)
    def _():
        for ch in range(C):
            for p, d in enumerate(order):
                if d:
                    remote(packed[ch], block(ch, c, y, p), send_sem.at[ch, 3], a_recv.at[ch, p],
                           at(s, y, (z + d) % nz, c)).start()
            held[ch][pl.ds(c * (ny * nz) + y * nz + own, 1)] = packed[ch][...]

    def turn(k, carry):
        g_copy(k).wait()
        turned[k] = greens[k].T
        return carry

    lax.fori_loop(0, kmax, turn, 0)
    s_copy.wait()
    solve_t[...] = solve[...].T
    f_copy.wait()

    for t in range(C + 2):
        if t < C:
            stage_a(t)
        if t >= 2:
            finish(t - 2)
        if 1 <= t <= C:
            stage_b(t - 1)

    def left(i, n):
        for ch in range(C):
            done(held[ch].at[pl.ds(0, n)], send_sem.at[ch, i])

    @pl.when(s == 0)
    def _():
        left(3, nz - 1)

    @pl.when(s < ns - 1)
    def _():
        left(0, nz)

    left(1, 3 * nz)
    left(2, ny * nz)


def shards(widths, ns, nrow, forcing, inflow, self_solve, greens, kept_cols, counts, name="sweep"):
    nz = nrow // (2 * NY)
    tile, columns = inflow.shape
    kmax = greens.shape[2]
    C = len(widths)
    smem = pl.BlockSpec(memory_space=pltpu.SMEM)
    hbm = pl.BlockSpec(memory_space=pltpu.HBM)
    dma = pltpu.SemaphoreType.DMA
    bf16 = jnp.bfloat16

    def chunk(n, w):
        return pltpu.VMEM((n, ROWS, tile * w // ROWS), bf16)

    out = pl.pallas_call(
        functools.partial(kernel, widths, ns, nz),
        name=name,
        out_shape=jax.ShapeDtypeStruct((columns, tile), jnp.float32),
        in_specs=[smem, smem, hbm, hbm, hbm, hbm],
        out_specs=pl.BlockSpec(memory_space=pltpu.VMEM),
        scratch_shapes=[
            *[chunk(2 * NY * nz, w) for w in widths],
            *[chunk(1, w) for w in widths],
            *[chunk(1, w) for w in widths],
            pltpu.VMEM((columns, tile), bf16),
            pltpu.VMEM((columns, tile), bf16),
            pltpu.VMEM((kmax, tile, tile), bf16),
            pltpu.VMEM((kmax, tile, tile), bf16),
            pltpu.VMEM((tile, tile), bf16),
            pltpu.VMEM((tile, tile), bf16),
            pltpu.SMEM((kmax,), jnp.int32),
            dma((3,)),
            dma((kmax,)),
            dma((C, nz)),
            dma((C, NY - 1, GROUPS)),
            dma((C, NY, GROUPS)),
            dma((C, 4)),
        ],
        compiler_params=pltpu.CompilerParams(
            collective_id=0, has_side_effects=True, vmem_limit_bytes=63 * 1024 * 1024
        ),
    )(kept_cols.reshape(kmax), counts.reshape(1), inflow.T, forcing[0].T, self_solve[0, 0], greens[0, 0])
    return out.astype(bf16).T[None]


def solution(mesh):
    placed = (
        P("slab", "row", None),
        P("row", None),
        P("slab", "row", None, None),
        P("slab", "row", None, None, None),
        P("slab", "row", None),
        P("slab", "row"),
    )
    return jax.shard_map(
        functools.partial(shards, WIDTHS, mesh.shape["slab"], mesh.shape["row"]),
        mesh=mesh, in_specs=placed, out_specs=P("slab", "row", None), check_vma=False,
    )
```

time: 409 us -> 84.8 us (0.21)
  waiting for transfers between devices: 324 us -> 0 us
  Pallas kernels: 0 us -> 82.5 us
  matrix products: 30.5 us -> 0 us
  local copies, waits for them, and re-layouts: 30.5 us -> 0 us
  between operations: 13.9 us -> 0.66 us
  starting transfers between devices: 5.43 us -> 0 us
    all_gather x4 -> x0, waiting for transfers between devices: 309 us -> none  [advance(): gathered = lax.all_gather(incoming, 'row', axis=0, tiled=True)]
    pallas_call x0 -> x1, Pallas kernels: none -> 82.5 us  [shards(): pl.pallas_call(functools.partial(kernel, widths, ns, nz), name=name, out_...]
    dot_general x4 -> x0, matrix products: 30.5 us -> none  [advance(): jnp.dot(solve_row, coupled, preferred_element_type=jnp.float32)]
    reshape x4 -> x0, local copies, waits for them, and re-layouts: 19.2 us -> none  [advance(): tiles = gathered.reshape(-1, TILE, width)]
    ppermute x4 -> x0, waiting for transfers between devices: 14.8 us -> none  [shifted(): return lax.ppermute(array, axis, pairs)]
    gather x4 -> x0, local copies, waits for them, and re-layouts: 11.3 us -> none  [advance(): chosen = tiles[cols_row]]
    ppermute x4 -> x0, starting transfers between devices: 5.3 us -> none  [shifted(): return lax.ppermute(array, axis, pairs)]
  transfers between devices with their start and end apart: 8 -> 0, of which waited for: 8 -> 0; matrix products, arithmetic and copies ran while one was open for 0% -> 0% of each run, Pallas kernels for 0% -> 0%
where the time goes in v3:
time: 84.8 us; the launch traced here: 84.7 us
  Pallas kernels  82.5 us (97%)
  other arithmetic  1.54 us (2%)
    pallas_call x1, Pallas kernels, shards(): pl.pallas_call(functools.partial(kernel, widths, ns, nz), name=name, out_...  82.5 us

profile of v3, /device:TPU:7, one launch (start us, length us, event | category | flops | bytes accessed | tf_op | source)
XLA Modules:
  0.0 84.7 jit_solution(2613708202487941635)
XLA Ops:
  0.7 82.5 %sweep.1 = f32[64,512]{1,0:T(8,128)} custom-call(s32[20]{0:T(128)} %bitcast.17, s32[1]{0:T(128)} %bitcast.12.count_ref, bf16[64,512]{1,0:T(8,128)(2,1)} %bitcast.15, bf16[64,512]{1,0:T(8,128)(2,1)} %bitcast.16, bf16[512,512]{1,0:T(8,128)(2,1)} %bitcast.14, bf16[20,512,512]{2,1,0:T(8,128)(2,1)} %bitcast.13), custom_call_target="tpu_custom_call" | custom-call | tf_op jit(solution)/shard_map/sweep/pallas_call | solution.py:234
  83.2 1.5 %convert_bitcast_fusion = bf16[1,512,64]{1,2,0:T(8,128)(2,1)} fusion(f32[64,512]{1,0:T(8,128)} %sweep.1), kind=kLoop, calls=%fused_computation | loop fusion | flops 32768 | bytes 196608 | tf_op jit(solution)/shard_map/broadcast_in_dim | solution.py:262
